TPU v7x, 512 devices: a whole 4x8x8 slice. The times are simulated.
512 devices in a mesh: lat: 32 (over x_hi, z, core), lon: 16 (over y, x_lo).
Axes of the slice: x: 4 (x_hi: 2, x_lo: 2; x = x_hi * 2 + x_lo), y: 8, z: 8, core: 2. Of those that a mesh axis runs over, the one named last changes fastest.
Arguments:
- nodes: bfloat16 [32, 16, 128, 512], P('lat', 'lon'), may hold values from -6 to 6
- top_nodes: bfloat16 [1024, 512], P('lat'), may hold values from -6 to 6
- cotangent: bfloat16 [32, 16, 128, 512], P('lat', 'lon'), may hold values from -3 to 3
- w_src: bfloat16 [512, 512], replicated, may hold values from -0.25 to 0.25
- w_dst: bfloat16 [512, 512], replicated, may hold values from -0.25 to 0.25
- w_msg: bfloat16 [512, 512], replicated, may hold values from -0.25 to 0.25
- w_top: bfloat16 [512, 512], replicated, may hold values from -0.25 to 0.25
- src_code: int32 [32, 16, 1024], P('lat', 'lon'), may hold values from 0 to 8
- src_node: int32 [32, 16, 1024], P('lat', 'lon'), may hold values from 0 to 127
- dst_node: int32 [32, 16, 1024], P('lat', 'lon'), may hold values from 0 to 127
- edge_count: int32 [32, 16], P('lat', 'lon'), may hold values from 256 to 1024, as said below
- parent: int32 [32, 16, 128], P('lat', 'lon'), may hold values from 0 to 1023, as said below
Outputs:
- updated: bfloat16 [32, 16, 128, 512], P('lat', 'lon')
- weight_grads: bfloat16 [4, 512, 512], replicated
- d_top: bfloat16 [1024, 512], P(('lat', 'lon'))
Inputs may be any that keep to these rules, and one draw needn't show every extreme that they name: `edge_count`: some block has all 1024 slots live. Top-level nodes come in bands of 32, one band for the one block row. Node n of block (i, j) lies at longitude position p = j * 128 + n, and c = p * 32 // 2048 is the band column above it. Its parent is (i) * 32 + k for a column k of 0 to 31 with |k - c| <= 2.
All inputs are finite; a program needn't handle non-finite values.
Results may differ from a plain program's by a relative error of at most 0.006.
Values may be sent and summed in bfloat16 or wider, within the bound.
No kernel may reach another device: no remote copies, remote signals or barrier semaphores. Data moves between devices by JAX's collectives and lax.ppermute only.
A program may use at most 64 MiB of HBM per device.

v0:
```python
import math
import jax
import jax.numpy as jnp
from jax import lax
from jax.sharding import PartitionSpec as P


def extended_2(block, sides, width):
    for axis, dim in sides:
        count = lax.axis_size(axis)
        forward = [(i, i + 1) for i in range(count - 1)]
        backward = [(target, source) for source, target in forward]
        low = lax.ppermute(
            lax.slice_in_dim(block, block.shape[dim] - width, None, axis=dim), axis, forward
        )
        high = lax.ppermute(lax.slice_in_dim(block, 0, width, axis=dim), axis, backward)
        block = jnp.concatenate([low, block, high], axis=dim)
    return block


def silu_slope(values):
    sigmoid_v = jax.nn.sigmoid(values)
    return sigmoid_v * (1.0 + values * (1.0 - sigmoid_v))


def contract_rows(left_mat, right_mat):
    return lax.dot_general(
        left_mat, right_mat, (((0,), (0,)), ((), ())), preferred_element_type=jnp.float32
    )


def shards(
    nodes,
    top_nodes,
    cotangent,
    w_src,
    w_dst,
    w_msg,
    w_top,
    src_code,
    src_node,
    dst_node,
    edge_count,
    parent,
):
    block_rows, block_cols, block_size, features = nodes.shape
    block_count = block_rows * block_cols
    slot_count = src_code.shape[-1]
    ext_cols = block_cols + 2
    top_local = top_nodes.shape[0]
    owner_rows = top_local // lax.axis_size("lon")
    lon_index = lax.axis_index("lon")
    band_start = lax.axis_index("lat") * top_local
    parents = parent.reshape(-1)
    band_ids = parents - band_start
    window_ids = band_ids - (lon_index - 1) * owner_rows
    top_table = jnp.dot(top_nodes, w_top, preferred_element_type=jnp.float32).astype(jnp.bfloat16)
    table_rows = jnp.take(top_table, band_ids, axis=0)
    extended = extended_2(nodes, (("lat", 0), ("lon", 1)), 1)
    ext_flat = extended.reshape(-1, features)
    src_proj = jnp.dot(ext_flat, w_src, preferred_element_type=jnp.float32)
    local_rows = nodes.reshape(-1, features)
    dst_proj = jnp.dot(local_rows, w_dst, preferred_element_type=jnp.float32)
    block_row = lax.iota(jnp.int32, block_rows)[:, None, None]
    block_col = lax.iota(jnp.int32, block_cols)[None, :, None]
    src_idx = (
        ((block_row + src_code // 3) * ext_cols + block_col + src_code % 3) * block_size + src_node
    ).reshape(-1)
    dst_idx = ((block_row * block_cols + block_col) * block_size + dst_node).reshape(-1)
    live_slot = lax.iota(jnp.int32, slot_count)[None, None, :] < edge_count[:, :, None]
    node_ids = lax.iota(jnp.int32, block_size)[None, :, None]
    one_hot = ((dst_node == node_ids) & live_slot).astype(jnp.bfloat16)
    pre_act = jnp.take(src_proj, src_idx, axis=0) + jnp.take(dst_proj, dst_idx, axis=0)
    hidden = jax.nn.silu(pre_act).astype(jnp.bfloat16)
    msg_pre = jnp.dot(hidden, w_msg, preferred_element_type=jnp.float32)
    message = jax.nn.silu(msg_pre).astype(jnp.bfloat16)
    inflow = jnp.einsum(
        "bne,bed->bnd",
        one_hot,
        message.reshape(block_count, slot_count, features),
        preferred_element_type=jnp.float32,
    ).reshape(-1, features)
    node_pre = inflow + table_rows.astype(jnp.float32)
    updated = (
        (local_rows.astype(jnp.float32) + jax.nn.silu(node_pre))
        .astype(jnp.bfloat16)
        .reshape(nodes.shape)
    )
    node_grad = (cotangent.reshape(-1, features).astype(jnp.float32) * silu_slope(node_pre)).astype(
        jnp.bfloat16
    )
    msg_grad = jnp.einsum(
        "bne,bnd->bed",
        one_hot,
        node_grad.reshape(block_count, block_size, features),
        preferred_element_type=jnp.float32,
    ).reshape(-1, features)
    pre_grad = (msg_grad * silu_slope(msg_pre)).astype(jnp.bfloat16)
    grad_msg = contract_rows(hidden, pre_grad)
    hidden_grad = lax.dot_general(
        pre_grad, w_msg, (((1,), (1,)), ((), ())), preferred_element_type=jnp.float32
    )
    act_grad = (hidden_grad * silu_slope(pre_act)).astype(jnp.bfloat16)
    dst_grad = (
        jnp.einsum(
            "bne,bed->bnd",
            one_hot,
            act_grad.reshape(block_count, slot_count, features),
            preferred_element_type=jnp.float32,
        )
        .astype(jnp.bfloat16)
        .reshape(-1, features)
    )
    grad_dst = contract_rows(local_rows, dst_grad)
    grad_src = contract_rows(jnp.take(ext_flat, src_idx, axis=0), act_grad)
    window_cols = lax.iota(jnp.int32, 3 * owner_rows)
    picks = (window_ids[:, None] == window_cols[None, :]).astype(jnp.bfloat16)
    window_sum = contract_rows(picks, node_grad)
    rims = jnp.concatenate([window_sum[:owner_rows], window_sum[2 * owner_rows :]], axis=0)
    rim_parts = extended_2(rims, (("lon", 0),), owner_rows)
    table_sum = (
        window_sum[owner_rows : 2 * owner_rows]
        + rim_parts[:owner_rows]
        + rim_parts[3 * owner_rows :]
    )
    table_grad = table_sum.astype(jnp.bfloat16)
    top_mine = lax.dynamic_slice_in_dim(top_nodes, lon_index * owner_rows, owner_rows, 0)
    d_top = lax.dot_general(
        table_grad, w_top, (((1,), (1,)), ((), ())), preferred_element_type=jnp.float32
    ).astype(jnp.bfloat16)
    grad_top = contract_rows(top_mine, table_grad)
    summed = lax.psum((grad_src, grad_dst, grad_msg, grad_top), ("lat", "lon"))
    nodes_total = block_count * block_size * lax.axis_size("lat") * lax.axis_size("lon")
    grad_scale = 8.0 / math.sqrt(nodes_total)
    weight_grads = (jnp.stack(summed) * grad_scale).astype(jnp.bfloat16)
    return (updated, weight_grads, d_top)


def solution(mesh):
    placed = (
        P("lat", "lon", None, None),
        P("lat", None),
        P("lat", "lon", None, None),
        P(),
        P(),
        P(),
        P(),
        P("lat", "lon", None),
        P("lat", "lon", None),
        P("lat", "lon", None),
        P("lat", "lon"),
        P("lat", "lon", None),
    )
    return jax.shard_map(
        shards,
        mesh=mesh,
        in_specs=placed,
        out_specs=(P("lat", "lon", None, None), P(), P(("lat", "lon"), None)),
        check_vma=False,
    )
```

profile of v0, /device:TPU:17, one launch (start us, length us, event | category | flops | bytes accessed | tf_op | source)
XLA Modules:
  0.0 388.7 jit_solution(804594889232757917)
XLA Ops:
  7.2 0.0 copy-start
  7.2 0.0 all-reduce.3.cloned.1.call-start
  7.2 2.7 collective-permute-start.1
  9.9 3.9 %collective-permute-start = (bf16[1,1,128,512]{3,2,1,0:T(8,128)(2,1)}, bf16[1,1,128,512]{3,2,1,0:T(8,128)(2,1)S(1)}, u32[]{:S(2)}, u32[]{:S(2)}) collective-permute-start(bf16[1,1,128,512]{3,2,1,0:T(8,128)(2,1)} %param.12), channel_id=1, source_target_pairs={{0,16},{16,32},{32,48},{48,64},{64,80},{80,96},{96,112},{112,128},... | collective-permute-start | bytes 393224 | tf_op jit(solution)/shard_map/ppermute | solution.py:13
  13.9 0.7 compare_select_fusion
  14.6 0.7 compare_select_fusion.1
  15.3 1.3 fusion.20
  16.7 0.7 fusion.28
  17.3 1.2 convolution_convert_fusion.1
  18.6 1.3 compare_and_fusion.2
  20.5 1.5 gather_fusion.2
  22.0 4.9 %gather_fusion.1 = f32[1024,512]{1,0:T(8,128)} fusion(f32[128,512]{1,0:T(8,128)S(1)} %fusion.20, s32[1024]{0:T(1024)S(1)} %get-tuple-element.14), kind=kCustom, calls=%fused_computation.1 | custom fusion | bytes 4198400 | tf_op jit(solution)/shard_map/jit(_take)/gather | solution.py:73
  26.9 0.6 iota_compare_fusion.3
  27.5 0.0 collective-permute-done.1
  27.5 3.0 collective-permute-start.3
  30.5 2.3 collective-permute-start.2
  32.8 0.5 bitcast_subtract_fusion
  33.4 14.3 %collective-permute-done.3 = bf16[3,1,128,512]{3,2,1,0:T(8,128)(2,1)S(1)} collective-permute-done((bf16[3,1,128,512]{3,2,1,0:T(8,128)(2,1)S(1)}, bf16[3,1,128,512]{3,2,1,0:T(8,128)(2,1)S(1)}, u32[]{:S(2)}, u32[]{:S(2)}) %collective-permute-start.3) | collective-permute-done | bytes 393248 | tf_op jit(solution)/shard_map/ppermute | solution.py:16
  47.7 0.3 collective-permute-done.2
  47.9 0.1 pad_maximum_fusion
  48.1 1.0 copy-done.1
  49.1 5.1 %gather_fusion.3 = bf16[1024,512]{1,0:T(8,128)(2,1)} fusion(bf16[1152,512]{1,0:T(8,128)(2,1)S(1)} %bitcast.58, s32[1024]{0:T(1024)S(1)} %broadcast_clamp_fusion.1), kind=kCustom, calls=%fused_computation.3 | custom fusion | bytes 2101248 | tf_op jit(solution)/shard_map/jit(_take)/gather | solution.py:115
  54.2 2.0 fusion.33
  56.2 4.9 %gather_fusion = f32[1024,512]{1,0:T(8,128)} fusion(f32[1152,512]{1,0:T(8,128)S(1)} %fusion.33, s32[1024]{0:T(1024)S(1)} %broadcast_clamp_fusion.1), kind=kCustom, calls=%fused_computation | custom fusion | bytes 4198400 | tf_op jit(solution)/shard_map/jit(_take)/gather | solution.py:73
  61.1 2.6 multiply_convert_fusion.3
  63.8 0.0 copy-start.8
  63.8 0.0 copy-start.11
  63.8 0.7 fusion.34
  64.5 0.2 copy-done.8
  64.7 1.5 fusion.10
  66.1 0.1 fusion.9
  66.3 0.0 copy-start.2
  66.3 0.9 multiply_convert_fusion.1
  67.2 0.7 copy-done.2
  67.8 0.6 copy-done.3
  68.5 1.6 multiply_convert_fusion
  70.1 1.7 convolution_bitcast_fusion.1
  71.9 0.2 fusion.22
  72.1 4.0 %collective-permute-start.4 = (f32[2,512]{1,0:T(2,128)S(1)}, f32[2,512]{1,0:T(2,128)S(1)}, u32[]{:S(2)}, u32[]{:S(2)}) collective-permute-start(f32[2,512]{1,0:T(2,128)S(1)} %get-tuple-element.9), channel_id=1, source_target_pairs={{0,1},{1,2},{2,3},{3,4},{4,5},{5,6},{6,7},{7,8},{8,9},{9,10},{10,1... | collective-permute-start | bytes 12296 | tf_op jit(solution)/shard_map/ppermute | solution.py:13
  76.1 2.2 collective-permute-start.5
  78.3 1.8 convolution_bitcast_fusion.3
  80.1 1.6 convolution_bitcast_fusion.2
  81.7 2.0 convolution_bitcast_fusion
  83.8 0.0 all-reduce.3.cloned.1.call-update
  83.8 1.0 copy-done.4
  84.8 0.8 convolution_convert_fusion.2
  85.6 292.2 %all-reduce.3.cloned.1.call-done = (f32[1,512,512]{2,1,0:T(8,128)}, f32[1,512,512]{2,1,0:T(8,128)}, f32[1,512,512]{2,1,0:T(8,128)}, f32[1,512,512]{2,1,0:T(8,128)}) async-done(((f32[1,512,512]{2,1,0:T(8,128)}, f32[1,512,512]{2,1,0:T(8,128)}, f32[1,512,512]{2,1,0:T(8,128)}, f32[1,512,512]{2,1,0:T(8,128)}), (f32[1,512,512]{2,1,0:T(8,128)}, f32[1,512,512]{2,1,0:T(8,128)}, f32[1,512,512]{2,1,0:T(8,128)}, ...) | async-done | bytes 4194320 | tf_op jit(solution)/shard_map/psum | solution.py:132
  377.8 4.1 %fusion = bf16[4,512,512]{2,1,0:T(8,128)(2,1)} fusion(f32[1,512,512]{2,1,0:T(8,128)} %get-tuple-element.3, f32[1,512,512]{2,1,0:T(8,128)} %get-tuple-element.4, f32[1,512,512]{2,1,0:T(8,128)} %get-tuple-element.5, f32[1,512,512]{2,1,0:T(8,128)} %get-tuple-element.6), kind=kLoop, calls=%fused_computation.5 | loop fusion | flops 5242880 | bytes 6291456 | tf_op jit(solution)/shard_map/convert_element_type | solution.py:135
  (32 shorter events, 0.1 us)
Async XLA Ops:
  7.2 56.6 %copy-start = (bf16[512,512]{1,0:T(8,128)(2,1)S(1)}, bf16[512,512]{1,0:T(8,128)(2,1)}, u32[]{:S(2)}) copy-start(bf16[512,512]{1,0:T(8,128)(2,1)} %param.17) | copy-start | bytes 1572868
  7.2 370.6 %all-reduce.3.cloned.1.call-start = ((), (), s32[]{:S(2)}) async-start(), calls=%async_computation | async-start | bytes 8388608 | tf_op jit(solution)/shard_map/psum | solution.py:132
  7.2 20.3 %collective-permute-start.1 = (bf16[1,1,128,512]{3,2,1,0:T(8,128)(2,1)}, bf16[1,1,128,512]{3,2,1,0:T(8,128)(2,1)S(1)}, u32[]{:S(2)}, u32[]{:S(2)}) collective-permute-start(bf16[1,1,128,512]{3,2,1,0:T(8,128)(2,1)} %param.12), channel_id=1, source_target_pairs={{16,0},{32,16},{48,32},{64,48},{80,64},{96,80},{112,96},{128,112},... | collective-permute-start | bytes 393224 | tf_op jit(solution)/shard_map/ppermute | solution.py:16
  9.9 17.5 %collective-permute-start = (bf16[1,1,128,512]{3,2,1,0:T(8,128)(2,1)}, bf16[1,1,128,512]{3,2,1,0:T(8,128)(2,1)S(1)}, u32[]{:S(2)}, u32[]{:S(2)}) collective-permute-start(bf16[1,1,128,512]{3,2,1,0:T(8,128)(2,1)} %param.12), channel_id=1, source_target_pairs={{0,16},{16,32},{32,48},{48,64},{64,80},{80,96},{96,112},{112,128},... | collective-permute-start | bytes 393224 | tf_op jit(solution)/shard_map/ppermute | solution.py:13
  22.0 5.5 %copy-start.5 = (bf16[1,1,128,512]{3,2,1,0:T(8,128)(2,1)S(1)}, bf16[1,1,128,512]{3,2,1,0:T(8,128)(2,1)}, u32[]{:S(2)}) copy-start(bf16[1,1,128,512]{3,2,1,0:T(8,128)(2,1)} %param.12) | copy-start | bytes 393220
  22.0 10.8 %copy-start.12 = (s32[1,1,128]{2,1,0:T(1,128)S(1)}, s32[1,1,128]{2,1,0:T(1,128)}, u32[]{:S(2)}) copy-start(s32[1,1,128]{2,1,0:T(1,128)} %param.23) | copy-start | bytes 1540
  22.0 11.3 %copy-start.10 = (s32[1,1,1024]{2,1,0:T(1,128)S(1)}, s32[1,1,1024]{2,1,0:T(1,128)}, u32[]{:S(2)}) copy-start(s32[1,1,1024]{2,1,0:T(1,128)} %param.21) | copy-start | bytes 12292
  27.5 20.1 %collective-permute-start.3 = (bf16[3,1,128,512]{3,2,1,0:T(8,128)(2,1)S(1)}, bf16[3,1,128,512]{3,2,1,0:T(8,128)(2,1)S(1)}, u32[]{:S(2)}, u32[]{:S(2)}) collective-permute-start(bf16[3,1,128,512]{3,2,1,0:T(8,128)(2,1)S(1)} %constant_dynamic-update-slice_fusion), channel_id=1, source_target_pairs={{1,0},{2,1},{3,2},{4,3},{5,4},{6,5},{7,6},{8,7},{9,8},{10,9},{11,1... | collective-permute-start | bytes 1179656 | tf_op jit(solution)/shard_map/ppermute | solution.py:16
  30.5 17.4 %collective-permute-start.2 = (bf16[3,1,128,512]{3,2,1,0:T(8,128)(2,1)S(1)}, bf16[3,1,128,512]{3,2,1,0:T(8,128)(2,1)S(1)}, u32[]{:S(2)}, u32[]{:S(2)}) collective-permute-start(bf16[3,1,128,512]{3,2,1,0:T(8,128)(2,1)S(1)} %constant_dynamic-update-slice_fusion), channel_id=1, source_target_pairs={{0,1},{1,2},{2,3},{3,4},{4,5},{5,6},{6,7},{7,8},{8,9},{9,10},{10,1... | collective-permute-start | bytes 1179656 | tf_op jit(solution)/shard_map/ppermute | solution.py:13
  48.1 1.0 copy-start.1
  49.1 5.1 %copy-start.7 = (bf16[512,512]{1,0:T(8,128)(2,1)S(1)}, bf16[512,512]{1,0:T(8,128)(2,1)}, u32[]{:S(2)}) copy-start(bf16[512,512]{1,0:T(8,128)(2,1)} %param.15) | copy-start | bytes 1572868
  63.8 0.9 copy-start.8
  63.8 0.9 copy-start.11
  63.8 0.9 copy-start.14
  64.7 1.5 copy-start.9
  66.3 1.6 copy-start.2
  66.3 2.2 copy-start.3
  70.1 1.8 copy-start.13
  70.1 8.2 %copy-start.6 = (bf16[1024,512]{1,0:T(8,128)(2,1)S(1)}, bf16[1024,512]{1,0:T(8,128)(2,1)}, u32[]{:S(2)}) copy-start(bf16[1024,512]{1,0:T(8,128)(2,1)} %gather_fusion.3) | copy-start | bytes 3145732
  72.1 9.6 %collective-permute-start.4 = (f32[2,512]{1,0:T(2,128)S(1)}, f32[2,512]{1,0:T(2,128)S(1)}, u32[]{:S(2)}, u32[]{:S(2)}) collective-permute-start(f32[2,512]{1,0:T(2,128)S(1)} %get-tuple-element.9), channel_id=1, source_target_pairs={{0,1},{1,2},{2,3},{3,4},{4,5},{5,6},{6,7},{7,8},{8,9},{9,10},{10,1... | collective-permute-start | bytes 12296 | tf_op jit(solution)/shard_map/ppermute | solution.py:13
  76.1 5.6 %collective-permute-start.5 = (f32[2,512]{1,0:T(2,128)S(1)}, f32[2,512]{1,0:T(2,128)S(1)}, u32[]{:S(2)}, u32[]{:S(2)}) collective-permute-start(f32[2,512]{1,0:T(2,128)S(1)} %get-tuple-element.10), channel_id=1, source_target_pairs={{1,0},{2,1},{3,2},{4,3},{5,4},{6,5},{7,6},{8,7},{9,8},{10,9},{11,1... | collective-permute-start | bytes 12296 | tf_op jit(solution)/shard_map/ppermute | solution.py:16
  83.7 1.0 copy-start.4
Sparse Core Ops, SparseCore 0:
  83.9 293.8 all-reduce.2
where the time goes:
time: 389 us
  waiting for transfers between devices  307 us (79%)
  local copies, waits for them, and re-layouts  19.9 us (5%)
  starting transfers between devices  18.1 us (5%)
  matrix products  17.5 us (4%)
  between operations  14.9 us (4%)
  other arithmetic  11.4 us (3%)
    psum x1, waiting for transfers between devices, shards(): summed = lax.psum((grad_src, grad_dst, grad_msg, grad_top), ('lat', 'lon'))  292 us
    ppermute x3, waiting for transfers between devices, extended_2(): lax.ppermute(lax.slice_in_dim(block, 0, width, axis=dim), axis, backward)  14.3 us
    ppermute x3, starting transfers between devices, extended_2(): lax.ppermute(lax.slice_in_dim(block, block.shape[dim] - width, None, axis...  10.2 us
    ppermute x3, starting transfers between devices, extended_2(): lax.ppermute(lax.slice_in_dim(block, 0, width, axis=dim), axis, backward)  7.93 us
  transfers between devices with their start and end apart: 7, of which 3 were waited for; matrix products, arithmetic and copies ran while one was open for 5% of the time, Pallas kernels for 0%

commit v1 on v0

--- a/solution.py
+++ b/solution.py
@@ -129,7 +129,9 @@
         table_grad, w_top, (((1,), (1,)), ((), ())), preferred_element_type=jnp.float32
     ).astype(jnp.bfloat16)
     grad_top = contract_rows(top_mine, table_grad)
-    summed = lax.psum((grad_src, grad_dst, grad_msg, grad_top), ("lat", "lon"))
+    summed = (grad_src, grad_dst, grad_msg, grad_top)
+    for name in ("lat", "lon"):
+        summed = lax.psum(summed, name)
     nodes_total = block_count * block_size * lax.axis_size("lat") * lax.axis_size("lon")
     grad_scale = 8.0 / math.sqrt(nodes_total)
     weight_grads = (jnp.stack(summed) * grad_scale).astype(jnp.bfloat16)

time: 389 us -> 598 us (1.54)
  the two profiles are of different devices: /device:TPU:17 before, /device:TPU:10 now
where the time goes in v1:
time: 598 us; the launch traced here: 597 us
  waiting for transfers between devices  516 us (86%)
  local copies, waits for them, and re-layouts  19.9 us (3%)
  matrix products  17.5 us (3%)
  starting transfers between devices  17.1 us (3%)
  between operations  15 us (3%)
  other arithmetic  11.4 us (2%)
    psum x2, waiting for transfers between devices, shards(): summed = lax.psum(summed, name)  500 us
    ppermute x3, waiting for transfers between devices, extended_2(): lax.ppermute(lax.slice_in_dim(block, 0, width, axis=dim), axis, backward)  12 us
  transfers between devices with their start and end apart: 8, of which 4 were waited for; matrix products, arithmetic and copies ran while one was open for 3% of the time, Pallas kernels for 0%

profile of v1, /device:TPU:10, one launch (start us, length us, event | category | flops | bytes accessed | tf_op | source)
XLA Modules:
  0.0 597.3 jit_solution(7446669781996171863)
XLA Ops:
  7.2 0.0 copy-start
  7.2 0.0 all-reduce.5.cloned.1.call-start
  7.2 1.4 collective-permute-start.1
  8.7 3.0 collective-permute-start
  11.7 0.7 compare_select_fusion
  12.4 0.7 compare_select_fusion.1
  13.2 1.3 fusion.21
  14.5 0.7 fusion.30
  15.2 1.2 convolution_convert_fusion.1
  16.4 1.3 compare_and_fusion.2
  18.4 1.5 gather_fusion.2
  19.9 4.9 gather_fusion.1
  24.7 0.6 iota_compare_fusion.3
  25.4 2.4 collective-permute-start.3
  27.8 4.3 collective-permute-start.2
  32.1 0.5 bitcast_subtract_fusion
  32.7 12.0 %collective-permute-done.3 = bf16[3,1,128,512]{3,2,1,0:T(8,128)(2,1)S(1)} collective-permute-done((bf16[3,1,128,512]{3,2,1,0:T(8,128)(2,1)S(1)}, bf16[3,1,128,512]{3,2,1,0:T(8,128)(2,1)S(1)}, u32[]{:S(2)}, u32[]{:S(2)}) %collective-permute-start.3) | collective-permute-done | bytes 393248 | tf_op jit(solution)/shard_map/ppermute | solution.py:16
  44.7 3.8 collective-permute-done.2
  48.5 0.1 pad_maximum_fusion
  48.7 1.0 copy-done.1
  49.7 5.1 gather_fusion.3
  54.7 2.0 fusion.35
  56.8 4.9 gather_fusion
  61.7 2.6 multiply_convert_fusion.3
  64.3 0.0 copy-start.11
  64.4 0.7 fusion.36
  65.1 0.2 copy-done.8
  65.3 1.5 fusion.11
  66.7 0.1 fusion.10
  66.9 0.9 multiply_convert_fusion.1
  67.8 0.7 copy-done.2
  68.4 0.6 copy-done.3
  69.1 1.6 multiply_convert_fusion
  70.7 1.7 fusion.37
  72.5 0.2 fusion.23
  72.7 2.5 collective-permute-start.4
  75.2 3.4 collective-permute-start.5
  78.6 1.8 fusion.1
  80.4 1.6 convolution_bitcast_fusion
  82.0 2.0 fusion.28
  84.0 0.0 all-reduce.5.cloned.1.call-update
  84.0 0.0 all-reduce.7.cloned.1.call-start
  84.1 290.3 %all-reduce.5.cloned.1.call-done = (f32[512,512]{1,0:T(8,128)}, f32[512,512]{1,0:T(8,128)}, f32[512,512]{1,0:T(8,128)}, f32[512,512]{1,0:T(8,128)}) async-done(((f32[512,512]{1,0:T(8,128)}, f32[512,512]{1,0:T(8,128)}, f32[512,512]{1,0:T(8,128)}, f32[512,512]{1,0:T(8,128)}), (f32[512,512]{1,0:T(8,128)}, f32[512,512]{1,0:T(8,128)}, f32[512,512]{1,0:T(8,128)}, ...) | async-done | bytes 4194320 | tf_op jit(solution)/shard_map/psum | solution.py:134
  374.3 0.0 all-reduce.7.cloned.1.call-update
  374.4 1.0 copy-done.4
  375.4 0.8 convolution_convert_fusion.2
  376.2 210.2 %all-reduce.7.cloned.1.call-done = (f32[1,512,512]{2,1,0:T(8,128)}, f32[1,512,512]{2,1,0:T(8,128)}, f32[1,512,512]{2,1,0:T(8,128)}, f32[1,512,512]{2,1,0:T(8,128)}) async-done(((f32[1,512,512]{2,1,0:T(8,128)}, f32[1,512,512]{2,1,0:T(8,128)}, f32[1,512,512]{2,1,0:T(8,128)}, f32[1,512,512]{2,1,0:T(8,128)}), (f32[1,512,512]{2,1,0:T(8,128)}, f32[1,512,512]{2,1,0:T(8,128)}, f32[1,512,512]{2,1,0:T(8,128)}, ...) | async-done | bytes 4194320 | tf_op jit(solution)/shard_map/psum | solution.py:134
  586.4 4.1 fusion
  (35 shorter events, 0.1 us)
Async XLA Ops:
  7.2 57.2 %copy-start = (bf16[512,512]{1,0:T(8,128)(2,1)S(1)}, bf16[512,512]{1,0:T(8,128)(2,1)}, u32[]{:S(2)}) copy-start(bf16[512,512]{1,0:T(8,128)(2,1)} %param.17) | copy-start | bytes 1572868
  7.2 367.2 %all-reduce.5.cloned.1.call-start = ((), (), s32[]{:S(2)}) async-start(), calls=%async_computation | async-start | bytes 8388608 | tf_op jit(solution)/shard_map/psum | solution.py:134
  7.2 18.1 %collective-permute-start.1 = (bf16[1,1,128,512]{3,2,1,0:T(8,128)(2,1)}, bf16[1,1,128,512]{3,2,1,0:T(8,128)(2,1)S(1)}, u32[]{:S(2)}, u32[]{:S(2)}) collective-permute-start(bf16[1,1,128,512]{3,2,1,0:T(8,128)(2,1)} %param.12), channel_id=1, source_target_pairs={{16,0},{32,16},{48,32},{64,48},{80,64},{96,80},{112,96},{128,112},... | collective-permute-start | bytes 393224 | tf_op jit(solution)/shard_map/ppermute | solution.py:16
  8.7 16.6 %collective-permute-start = (bf16[1,1,128,512]{3,2,1,0:T(8,128)(2,1)}, bf16[1,1,128,512]{3,2,1,0:T(8,128)(2,1)S(1)}, u32[]{:S(2)}, u32[]{:S(2)}) collective-permute-start(bf16[1,1,128,512]{3,2,1,0:T(8,128)(2,1)} %param.12), channel_id=1, source_target_pairs={{0,16},{16,32},{32,48},{48,64},{64,80},{80,96},{96,112},{112,128},... | collective-permute-start | bytes 393224 | tf_op jit(solution)/shard_map/ppermute | solution.py:13
  19.9 5.5 copy-start.5
  19.9 12.3 %copy-start.12 = (s32[1,1,128]{2,1,0:T(1,128)S(1)}, s32[1,1,128]{2,1,0:T(1,128)}, u32[]{:S(2)}) copy-start(s32[1,1,128]{2,1,0:T(1,128)} %param.23) | copy-start | bytes 1540
  19.9 12.8 %copy-start.10 = (s32[1,1,1024]{2,1,0:T(1,128)S(1)}, s32[1,1,1024]{2,1,0:T(1,128)}, u32[]{:S(2)}) copy-start(s32[1,1,1024]{2,1,0:T(1,128)} %param.21) | copy-start | bytes 12292
  25.4 19.3 %collective-permute-start.3 = (bf16[3,1,128,512]{3,2,1,0:T(8,128)(2,1)S(1)}, bf16[3,1,128,512]{3,2,1,0:T(8,128)(2,1)S(1)}, u32[]{:S(2)}, u32[]{:S(2)}) collective-permute-start(bf16[3,1,128,512]{3,2,1,0:T(8,128)(2,1)S(1)} %constant_dynamic-update-slice_fusion), channel_id=1, source_target_pairs={{1,0},{2,1},{3,2},{4,3},{5,4},{6,5},{7,6},{8,7},{9,8},{10,9},{11,1... | collective-permute-start | bytes 1179656 | tf_op jit(solution)/shard_map/ppermute | solution.py:16
  27.8 20.7 %collective-permute-start.2 = (bf16[3,1,128,512]{3,2,1,0:T(8,128)(2,1)S(1)}, bf16[3,1,128,512]{3,2,1,0:T(8,128)(2,1)S(1)}, u32[]{:S(2)}, u32[]{:S(2)}) collective-permute-start(bf16[3,1,128,512]{3,2,1,0:T(8,128)(2,1)S(1)} %constant_dynamic-update-slice_fusion), channel_id=1, source_target_pairs={{0,1},{1,2},{2,3},{3,4},{4,5},{5,6},{6,7},{7,8},{8,9},{9,10},{10,1... | collective-permute-start | bytes 1179656 | tf_op jit(solution)/shard_map/ppermute | solution.py:13
  48.6 1.0 copy-start.1
  49.7 5.1 copy-start.7
  64.3 0.9 copy-start.8
  64.3 0.9 copy-start.11
  64.4 0.9 copy-start.14
  65.2 1.5 copy-start.9
  66.8 1.6 copy-start.2
  66.8 2.2 copy-start.3
  70.7 1.8 copy-start.13
  70.7 7.9 %copy-start.6 = (bf16[1024,512]{1,0:T(8,128)(2,1)S(1)}, bf16[1024,512]{1,0:T(8,128)(2,1)}, u32[]{:S(2)}) copy-start(bf16[1024,512]{1,0:T(8,128)(2,1)} %gather_fusion.3) | copy-start | bytes 3145732
  72.7 9.2 %collective-permute-start.4 = (f32[2,512]{1,0:T(2,128)S(1)}, f32[2,512]{1,0:T(2,128)S(1)}, u32[]{:S(2)}, u32[]{:S(2)}) collective-permute-start(f32[2,512]{1,0:T(2,128)S(1)} %get-tuple-element.13), channel_id=1, source_target_pairs={{0,1},{1,2},{2,3},{3,4},{4,5},{5,6},{6,7},{7,8},{8,9},{9,10},{10,1... | collective-permute-start | bytes 12296 | tf_op jit(solution)/shard_map/ppermute | solution.py:13
  75.2 6.8 %collective-permute-start.5 = (f32[2,512]{1,0:T(2,128)S(1)}, f32[2,512]{1,0:T(2,128)S(1)}, u32[]{:S(2)}, u32[]{:S(2)}) collective-permute-start(f32[2,512]{1,0:T(2,128)S(1)} %get-tuple-element.14), channel_id=1, source_target_pairs={{1,0},{2,1},{3,2},{4,3},{5,4},{6,5},{7,6},{8,7},{9,8},{10,9},{11,1... | collective-permute-start | bytes 12296 | tf_op jit(solution)/shard_map/ppermute | solution.py:16
  84.0 502.4 %all-reduce.7.cloned.1.call-start = ((), (), s32[]{:S(2)}) async-start(), calls=%async_computation.1 | async-start | bytes 8388608 | tf_op jit(solution)/shard_map/psum | solution.py:134
  374.3 1.0 copy-start.4
Sparse Core Ops, SparseCore 0:
  84.1 290.1 all-reduce.4
  377.5 208.8 all-reduce.6
